TPU v7x, 128 devices: a whole 4x4x4 slice. The times are simulated.
128 devices in a mesh: row: 16 (over y, x), col: 8 (over z, core).
Axes of the slice: x: 4, y: 4, z: 4, core: 2. Of those that a mesh axis runs over, the one named last changes fastest.
Arguments:
- orbitals: float32 [32768, 1024], P('row', 'col'), may hold values from -6 to 6
- point_index: int32 [8192], replicated, may hold values from 0 to 32767, as said below
- coulomb: float32 [8192, 8192], P('row', 'col'), may hold values from -0.001953125 to 0.001953125
- fitting: float32 [32768, 8192], P('row', 'col'), may hold values from -0.0625 to 0.0625
Outputs:
- exchange_out: float32 [32768, 1024], P('row', 'col')
Inputs may be any that keep to these rules, and one draw needn't show every extreme that they name: `point_index`: indices are distinct. Grid index g lies in slab g // 2048. Of the 512 consecutive points of each row panel, at most 64 lie in one slab, and in every panel exactly 64 lie in one slab.
All inputs are finite; a program needn't handle non-finite values.
Results may differ from a plain program's by a relative error of at most 0.00012.
Values sent between devices are 32-bit elements; how exact they have to be, the bound alone decides.
No kernel may reach another device: no remote copies, remote signals or barrier semaphores. Data moves between devices by JAX's collectives and lax.ppermute only.
A program may use at most 64 MiB of HBM per device.

v0:
```python
import jax
import jax.numpy as jnp
from jax import lax
from jax.sharding import PartitionSpec as P


def per_device(orbitals, point_index, coulomb, fitting):
    row_count = lax.axis_size("row")
    slab_rows = orbitals.shape[0]
    band_cols = orbitals.shape[1]
    total_points = point_index.shape[0]
    per_panel = total_points // row_count
    slot_count = 2 * per_panel // row_count
    my_row = lax.axis_index("row")
    my_col = lax.axis_index("col")
    owner = point_index // slab_rows
    local_row = point_index - owner * slab_rows
    owner_grid = owner.reshape(row_count, per_panel)
    local_grid = local_row.reshape(row_count, per_panel)
    matches = (owner_grid[:, :, None] == jnp.arange(row_count)[None, None, :]).astype(jnp.int32)
    ranking = jnp.cumsum(matches, axis=1) - 1
    slot_grid = jnp.sum(jnp.where(matches > 0, ranking, 0), axis=2)
    mine = owner_grid == my_row
    chosen = mine[:, :, None] & (slot_grid[:, :, None] == jnp.arange(slot_count)[None, None, :])
    source_row = jnp.sum(jnp.where(chosen, local_grid[:, :, None], 0), axis=1)
    valid = jnp.any(chosen, axis=1)
    outgoing = jnp.where(valid[:, :, None], orbitals[source_row], 0.0)
    received = lax.all_to_all(outgoing, "row", split_axis=0, concat_axis=0, tiled=True)
    flattened = received.reshape(row_count * slot_count, band_cols)
    owner_mine = lax.dynamic_slice_in_dim(owner_grid, my_row, 1, 0)[0]
    slot_mine = lax.dynamic_slice_in_dim(slot_grid, my_row, 1, 0)[0]
    panel_strip = flattened[owner_mine * slot_count + slot_mine]
    panel_full = lax.all_gather(panel_strip, "col", axis=1, tiled=True)
    strip_all = lax.all_gather(panel_strip, "row", axis=0, tiled=True)
    column_full = lax.all_to_all(strip_all, "col", split_axis=0, concat_axis=1, tiled=True)
    pair = jnp.dot(
        panel_full,
        column_full.T,
        precision=lax.Precision.HIGHEST,
        preferred_element_type=jnp.float32,
    )
    partial_value = jnp.dot(
        coulomb * pair,
        column_full,
        precision=lax.Precision.HIGHEST,
        preferred_element_type=jnp.float32,
    )
    summed = lax.psum(partial_value, "col")
    weight_strip = lax.dynamic_slice_in_dim(summed, my_col * band_cols, band_cols, 1)
    weight_all = lax.all_gather(weight_strip, "row", axis=0, tiled=True)
    weight_column = lax.all_to_all(weight_all, "col", split_axis=0, concat_axis=1, tiled=True)
    term = -jnp.dot(
        fitting, weight_column, precision=lax.Precision.HIGHEST, preferred_element_type=jnp.float32
    )
    return lax.psum_scatter(term, "col", scatter_dimension=1, tiled=True)


def solution(mesh):
    in_specs = (P("row", "col"), P(), P("row", "col"), P("row", "col"))
    out_specs = P("row", "col")
    return jax.shard_map(
        per_device, mesh=mesh, in_specs=in_specs, out_specs=out_specs, check_vma=False
    )
```

profile of v0, /device:TPU:1, one launch (start us, length us, event | category | flops | bytes accessed | tf_op | source)
XLA Modules:
  0.0 455.0 jit_solution(17053227646644260959)
XLA Ops:
  6.5 0.0 copy-start
  6.5 0.9 add_select_fusion
  7.4 0.1 fusion.6
  7.5 18.1 %reduce-window.6 = s32[16,16,4,128]{3,1,2,0:T(8,128)S(1)} reduce-window(s32[16,16,4,128]{3,1,2,0:T(8,128)S(1)} %fusion.6, s32[]{:T(128)} %constant.16.clone.1), window={size=1x1x1x128 pad=0_0x0_0x0_0x127_0}, to_apply=%region_0.1 | reduce-window | flops 16646144 | bytes 1048580 | tf_op jit(solution)/shard_map/reduce-window
  25.6 0.2 slice.12
  25.9 0.4 copy.12
  26.3 0.1 fusion.8
  26.5 0.2 fusion.5
  26.7 0.4 fusion.3
  27.1 0.5 select_reduce_fusion
  27.7 0.1 reshape.84
  27.7 0.0 copy-done
  27.7 2.8 gather_fusion
  30.6 1.0 broadcast_select_fusion
  31.6 7.6 %all-to-all-start = ((f32[16,64,128]{2,1,0:T(8,128)}), f32[16,64,128]{2,1,0:T(8,128)S(1)}, u32[]{:S(2)}, u32[]{:S(2)}) async-start(f32[16,64,128]{2,1,0:T(8,128)} %broadcast_select_fusion), calls=%async_computation | async-start | bytes 1048576 | tf_op jit(solution)/shard_map/all_to_all | solution.py:28
  39.1 0.0 all-gather.10.cloned.1.call-start
  39.2 10.3 %all-to-all-done = f32[16,64,128]{2,1,0:T(8,128)S(1)} async-done(((f32[16,64,128]{2,1,0:T(8,128)}), f32[16,64,128]{2,1,0:T(8,128)S(1)}, u32[]{:S(2)}, u32[]{:S(2)}) %all-to-all-start) | async-done | bytes 524320 | tf_op jit(solution)/shard_map/all_to_all | solution.py:28
  49.6 1.6 gather_fusion.1
  51.2 0.0 all-gather.10.cloned.1.call-update
  51.2 0.0 all-gather.8.cloned.1.call-start
  51.3 0.7 all-gather.8.cloned.1.call-update
  52.0 50.4 %all-gather.10.cloned.1.call-done = f32[8192,128]{1,0:T(8,128)} async-done(((f32[512,128]{1,0:T(8,128)}), f32[8192,128]{1,0:T(8,128)}) %all-gather.10.cloned.1.call-update) | async-done | bytes 4194320 | tf_op jit(solution)/shard_map/all_gather | solution.py:34
  102.4 5.4 %copy.15 = f32[8,1024,128]{1,2,0:T(8,128)} copy(f32[8,1024,128]{2,1,0:T(8,128)} %bitcast.44) | data formatting | bytes 8388608 | tf_op jit(solution)/shard_map/all_to_all | solution.py:35
  107.7 5.3 %all-to-all-start.1 = ((f32[8,1024,128]{1,2,0:T(8,128)}), f32[8,1024,128]{1,2,0:T(8,128)}, u32[]{:S(2)}, u32[]{:S(2)}) async-start(f32[8,1024,128]{1,2,0:T(8,128)} %copy.15), calls=%async_computation.1 | async-start | bytes 8388608 | tf_op jit(solution)/shard_map/all_to_all | solution.py:35
  113.0 0.0 all-reduce.2.cloned.1.call-start
  113.0 31.5 %all-gather.8.cloned.1.call-done = f32[512,1024]{1,0:T(8,128)} async-done(((f32[512,128]{1,0:T(8,128)}), f32[512,1024]{1,0:T(8,128)}) %all-gather.8.cloned.1.call-update) | async-done | bytes 2097168 | tf_op jit(solution)/shard_map/all_gather | solution.py:33
  144.5 25.7 %all-to-all-done.1 = f32[8,1024,128]{1,2,0:T(8,128)} async-done(((f32[8,1024,128]{1,2,0:T(8,128)}), f32[8,1024,128]{1,2,0:T(8,128)}, u32[]{:S(2)}, u32[]{:S(2)}) %all-to-all-start.1) | async-done | bytes 4194336 | tf_op jit(solution)/shard_map/all_to_all | solution.py:35
  170.2 0.0 copy-start.1
  170.2 9.8 %fusion.11 = f32[512,1024]{1,0:T(8,128)S(1)} fusion(f32[512,1024]{1,0:T(8,128)} %all-gather.8.cloned.1.call-done, f32[1024,1024]{0,1:T(8,128)} %bitcast.10), kind=kOutput, calls=%fused_computation.34 | convolution fusion | flops 6442450944 | bytes 8388608 | tf_op jit(solution)/shard_map/dot_general | solution.py:36
  180.0 0.0 copy-done.1
  180.0 9.8 %fusion = f32[512,1024]{1,0:T(8,128)} fusion(f32[1024,1024]{0,1:T(8,128)} %bitcast.10, f32[512,1024]{1,0:T(8,128)S(1)} %copy-done.1, f32[512,1024]{1,0:T(8,128)S(1)} %fusion.11), kind=kOutput, calls=%fused_computation.3 | convolution fusion | flops 6442975232 | bytes 10485760 | tf_op jit(solution)/shard_map/dot_general | solution.py:42
  189.8 0.0 all-reduce.2.cloned.1.call-update
  189.8 0.0 all-gather.6.cloned.1.call-start
  189.9 62.2 %all-reduce.2.cloned.1.call-done = f32[512,1024]{1,0:T(8,128)} async-done(((f32[512,1024]{1,0:T(8,128)}), f32[512,1024]{1,0:T(8,128)}) %all-reduce.2.cloned.1.call-update) | async-done | bytes 2097168 | tf_op jit(solution)/shard_map/psum | solution.py:48
  252.1 1.7 constant_dynamic-slice_fusion
  253.7 0.0 all-gather.6.cloned.1.call-update
  253.7 0.0 reduce-scatter.2.cloned.1.call-start
  253.8 52.7 %all-gather.6.cloned.1.call-done = f32[8192,128]{1,0:T(8,128)} async-done(((f32[512,128]{1,0:T(8,128)}), f32[8192,128]{1,0:T(8,128)}) %all-gather.6.cloned.1.call-update) | async-done | bytes 4194320 | tf_op jit(solution)/shard_map/all_gather | solution.py:50
  306.5 5.4 %copy.16 = f32[8,1024,128]{1,2,0:T(8,128)} copy(f32[8,1024,128]{2,1,0:T(8,128)} %bitcast.45) | data formatting | bytes 8388608 | tf_op jit(solution)/shard_map/all_to_all | solution.py:51
  311.9 53.9 %all_to_all.43 = f32[8,1024,128]{1,2,0:T(8,128)S(1)} all-to-all(f32[8,1024,128]{1,2,0:T(8,128)} %copy.16), channel_id=1, replica_groups=mesh['row'=16,'col'=8] {'col'}, dimensions={0} | all-to-all | bytes 8388608 | tf_op jit(solution)/shard_map/all_to_all | solution.py:51
  365.8 29.9 %negate_bitcast_fusion = f32[2048,1024]{0,1:T(8,128)} fusion(f32[1024,1024]{0,1:T(8,128)S(1)} %bitcast.46, f32[2048,1024]{1,0:T(8,128)} %param.7), kind=kOutput, calls=%fused_computation.2 | convolution fusion | flops 25771900928 | bytes 20971520 | tf_op jit(solution)/shard_map/dot_general | solution.py:52
  395.6 0.0 reduce-scatter.2.cloned.1.call-update
  395.7 50.2 %reduce-scatter.2.cloned.1.call-done = f32[2048,128]{0,1:T(8,128)} async-done(((f32[2048,1024]{0,1:T(8,128)}), f32[2048,128]{0,1:T(8,128)}) %reduce-scatter.2.cloned.1.call-update) | async-done | bytes 1048592 | tf_op jit(solution)/shard_map/reduce_scatter | solution.py:55
  445.9 2.5 copy.17
  (9 shorter events, 0.1 us)
Async XLA Ops:
  6.5 21.2 %copy-start = (f32[2048,128]{1,0:T(8,128)S(1)}, f32[2048,128]{1,0:T(8,128)}, u32[]{:S(2)}) copy-start(f32[2048,128]{1,0:T(8,128)} %param.4) | copy-start | bytes 3145732
  31.6 18.0 %all-to-all-start = ((f32[16,64,128]{2,1,0:T(8,128)}), f32[16,64,128]{2,1,0:T(8,128)S(1)}, u32[]{:S(2)}, u32[]{:S(2)}) async-start(f32[16,64,128]{2,1,0:T(8,128)} %broadcast_select_fusion), calls=%async_computation | async-start | bytes 1048576 | tf_op jit(solution)/shard_map/all_to_all | solution.py:28
  39.1 63.2 %all-gather.10.cloned.1.call-start = ((), (), s32[]{:S(2)}) async-start(), calls=%async_computation.8 | async-start | bytes 4456448 | tf_op jit(solution)/shard_map/all_gather | solution.py:34
  51.2 93.3 %all-gather.8.cloned.1.call-start = ((), (), s32[]{:S(2)}) async-start(), calls=%async_computation.7 | async-start | bytes 2359296 | tf_op jit(solution)/shard_map/all_gather | solution.py:33
  107.7 62.5 %all-to-all-start.1 = ((f32[8,1024,128]{1,2,0:T(8,128)}), f32[8,1024,128]{1,2,0:T(8,128)}, u32[]{:S(2)}, u32[]{:S(2)}) async-start(f32[8,1024,128]{1,2,0:T(8,128)} %copy.15), calls=%async_computation.1 | async-start | bytes 8388608 | tf_op jit(solution)/shard_map/all_to_all | solution.py:35
  113.0 139.1 %all-reduce.2.cloned.1.call-start = ((), (), s32[]{:S(2)}) async-start(), calls=%async_computation.4 | async-start | bytes 4194304 | tf_op jit(solution)/shard_map/psum | solution.py:48
  170.2 9.8 %copy-start.1 = (f32[512,1024]{1,0:T(8,128)S(1)}, f32[512,1024]{1,0:T(8,128)}, u32[]{:S(2)}) copy-start(f32[512,1024]{1,0:T(8,128)} %param.6) | copy-start | bytes 6291460
  189.8 116.7 %all-gather.6.cloned.1.call-start = ((), (), s32[]{:S(2)}) async-start(), calls=%async_computation.5 | async-start | bytes 4456448 | tf_op jit(solution)/shard_map/all_gather | solution.py:50
  253.7 192.2 %reduce-scatter.2.cloned.1.call-start = ((), (), s32[]{:S(2)}) async-start(), calls=%async_computation.6 | async-start | bytes 9437184 | tf_op jit(solution)/shard_map/reduce_scatter | solution.py:55
Sparse Core Ops, SparseCore 0:
  51.3 50.9 all-gather.9
  104.0 40.3 all-gather.7
  190.0 62.0 all-reduce.1
  254.1 52.4 all-gather.5
  395.8 50.0 reduce-scatter.1
where the time goes:
time: 456 us; the launch traced here: 455 us
  waiting for transfers between devices  284 us (62%)
  blocking collectives  53.9 us (12%)
  matrix products  49.4 us (11%)
  other arithmetic  21.4 us (5%)
  local copies, waits for them, and re-layouts  20.1 us (4%)
  between operations  13.3 us (3%)
  starting transfers between devices  13 us (3%)
    psum x1, waiting for transfers between devices, per_device(): summed = lax.psum(partial_value, 'col')  62.2 us
    all_to_all x1, blocking collectives, per_device(): lax.all_to_all(weight_all, 'col', split_axis=0, concat_axis=1, tiled=True)  53.9 us
    all_gather x1, waiting for transfers between devices, per_device(): weight_all = lax.all_gather(weight_strip, 'row', axis=0, tiled=True)  52.7 us
    all_gather x1, waiting for transfers between devices, per_device(): strip_all = lax.all_gather(panel_strip, 'row', axis=0, tiled=True)  50.4 us
    reduce_scatter x1, waiting for transfers between devices, per_device(): return lax.psum_scatter(term, 'col', scatter_dimension=1, tiled=True)  50.2 us
    all_gather x1, waiting for transfers between devices, per_device(): panel_full = lax.all_gather(panel_strip, 'col', axis=1, tiled=True)  31.5 us
    dot_general x1, matrix products, per_device(): jnp.dot(fitting, weight_column, precision=lax.Precision.HIGHEST, preferre...  29.9 us
    all_to_all x1, waiting for transfers between devices, per_device(): lax.all_to_all(strip_all, 'col', split_axis=0, concat_axis=1, tiled=True)  25.7 us
  transfers between devices with their start and end apart: 7, of which 7 were waited for; matrix products, arithmetic and copies ran while one was open for 1% of the time, Pallas kernels for 0%

commit v1 on v0

--- a/solution.py
+++ b/solution.py
@@ -2,6 +2,7 @@
 import jax.numpy as jnp
 from jax import lax
 from jax.sharding import PartitionSpec as P
+from jax.lax import all_to_all, axis_size
 
 
 def per_device(orbitals, point_index, coulomb, fitting):
@@ -47,7 +48,9 @@
     )
     summed = lax.psum(partial_value, "col")
     weight_strip = lax.dynamic_slice_in_dim(summed, my_col * band_cols, band_cols, 1)
-    weight_all = lax.all_gather(weight_strip, "row", axis=0, tiled=True)
+    weight_all = jnp.concatenate(
+        all_to_all(jnp.stack([weight_strip] * axis_size("row")), "row", 0, 0), 0
+    )
     weight_column = lax.all_to_all(weight_all, "col", split_axis=0, concat_axis=1, tiled=True)
     term = -jnp.dot(
         fitting, weight_column, precision=lax.Precision.HIGHEST, preferred_element_type=jnp.float32

time: 456 us -> 460 us (level)
  blocking collectives: 53.9 us -> 113 us
  waiting for transfers between devices: 284 us -> 229 us
    all_to_all x0 -> x1, blocking collectives: none -> 54.8 us  [per_device(): all_to_all(jnp.stack([weight_strip] * axis_size('row')), 'row', 0, 0)]
    all_gather x1 -> x0, waiting for transfers between devices: 52.7 us -> none  [per_device(): weight_all = lax.all_gather(weight_strip, 'row', axis=0, tiled=True)]
  transfers between devices with their start and end apart: 7 -> 6, of which waited for: 7 -> 6; matrix products, arithmetic and copies ran while one was open for 1% -> 1% of each run, Pallas kernels for 0% -> 0%
where the time goes in v1:
time: 460 us
  waiting for transfers between devices  229 us (50%)
  blocking collectives  113 us (25%)
  matrix products  50.6 us (11%)
  other arithmetic  21.4 us (5%)
  local copies, waits for them, and re-layouts  19.8 us (4%)
  between operations  13.3 us (3%)
  starting transfers between devices  13 us (3%)
    psum x1, waiting for transfers between devices, per_device(): summed = lax.psum(partial_value, 'col')  62.2 us
    all_to_all x1, blocking collectives, per_device(): lax.all_to_all(weight_all, 'col', split_axis=0, concat_axis=1, tiled=True)  57.9 us
    all_to_all x1, blocking collectives, per_device(): all_to_all(jnp.stack([weight_strip] * axis_size('row')), 'row', 0, 0)  54.8 us
    all_gather x1, waiting for transfers between devices, per_device(): strip_all = lax.all_gather(panel_strip, 'row', axis=0, tiled=True)  50.4 us
    reduce_scatter x1, waiting for transfers between devices, per_device(): return lax.psum_scatter(term, 'col', scatter_dimension=1, tiled=True)  48 us
    all_gather x1, waiting for transfers between devices, per_device(): panel_full = lax.all_gather(panel_strip, 'col', axis=1, tiled=True)  31.5 us
    dot_general x1, matrix products, per_device(): jnp.dot(fitting, weight_column, precision=lax.Precision.HIGHEST, preferre...  31 us
    all_to_all x1, waiting for transfers between devices, per_device(): lax.all_to_all(strip_all, 'col', split_axis=0, concat_axis=1, tiled=True)  25.7 us
  transfers between devices with their start and end apart: 6, of which 6 were waited for; matrix products, arithmetic and copies ran while one was open for 1% of the time, Pallas kernels for 0%

profile of v1, /device:TPU:1, one launch (start us, length us, event | category | flops | bytes accessed | tf_op | source)
XLA Modules:
  0.0 459.6 jit_solution(10626325815664863191)
XLA Ops:
  6.5 0.0 copy-start
  6.5 0.9 add_select_fusion
  7.4 0.1 fusion.6
  7.5 18.1 %reduce-window.6 = s32[16,16,4,128]{3,1,2,0:T(8,128)S(1)} reduce-window(s32[16,16,4,128]{3,1,2,0:T(8,128)S(1)} %fusion.6, s32[]{:T(128)} %constant.16.clone.1), window={size=1x1x1x128 pad=0_0x0_0x0_0x127_0}, to_apply=%region_0.1 | reduce-window | flops 16646144 | bytes 1048580 | tf_op jit(solution)/shard_map/reduce-window
  25.6 0.2 slice.12
  25.9 0.4 copy.17
  26.3 0.1 fusion.8
  26.5 0.2 fusion.5
  26.7 0.4 fusion.3
  27.1 0.5 select_reduce_fusion
  27.7 0.1 reshape.88
  27.7 0.0 copy-done
  27.7 2.8 gather_fusion
  30.6 1.0 broadcast_select_fusion
  31.6 7.6 %all-to-all-start = ((f32[16,64,128]{2,1,0:T(8,128)}), f32[16,64,128]{2,1,0:T(8,128)S(1)}, u32[]{:S(2)}, u32[]{:S(2)}) async-start(f32[16,64,128]{2,1,0:T(8,128)} %broadcast_select_fusion), calls=%async_computation | async-start | bytes 1048576 | tf_op jit(solution)/shard_map/all_to_all | solution.py:29
  39.1 0.0 all-gather.7.cloned.1.call-start
  39.2 10.3 %all-to-all-done = f32[16,64,128]{2,1,0:T(8,128)S(1)} async-done(((f32[16,64,128]{2,1,0:T(8,128)}), f32[16,64,128]{2,1,0:T(8,128)S(1)}, u32[]{:S(2)}, u32[]{:S(2)}) %all-to-all-start) | async-done | bytes 524320 | tf_op jit(solution)/shard_map/all_to_all | solution.py:29
  49.6 1.6 gather_fusion.1
  51.2 0.0 all-gather.7.cloned.1.call-update
  51.2 0.0 all-gather.5.cloned.1.call-start
  51.3 0.7 all-gather.5.cloned.1.call-update
  52.0 50.4 %all-gather.7.cloned.1.call-done = f32[8192,128]{1,0:T(8,128)} async-done(((f32[512,128]{1,0:T(8,128)}), f32[8192,128]{1,0:T(8,128)}) %all-gather.7.cloned.1.call-update) | async-done | bytes 4194320 | tf_op jit(solution)/shard_map/all_gather | solution.py:35
  102.4 5.3 %copy.20 = f32[8,1024,128]{1,2,0:T(8,128)} copy(f32[8,1024,128]{2,1,0:T(8,128)} %bitcast.45) | data formatting | bytes 8388608 | tf_op jit(solution)/shard_map/all_to_all | solution.py:36
  107.7 5.3 %all-to-all-start.1 = ((f32[8,1024,128]{1,2,0:T(8,128)}), f32[8,1024,128]{1,2,0:T(8,128)}, u32[]{:S(2)}, u32[]{:S(2)}) async-start(f32[8,1024,128]{1,2,0:T(8,128)} %copy.20), calls=%async_computation.1 | async-start | bytes 8388608 | tf_op jit(solution)/shard_map/all_to_all | solution.py:36
  113.0 0.0 all-reduce.2.cloned.1.call-start
  113.0 31.5 %all-gather.5.cloned.1.call-done = f32[512,1024]{1,0:T(8,128)} async-done(((f32[512,128]{1,0:T(8,128)}), f32[512,1024]{1,0:T(8,128)}) %all-gather.5.cloned.1.call-update) | async-done | bytes 2097168 | tf_op jit(solution)/shard_map/all_gather | solution.py:34
  144.5 25.7 %all-to-all-done.1 = f32[8,1024,128]{1,2,0:T(8,128)} async-done(((f32[8,1024,128]{1,2,0:T(8,128)}), f32[8,1024,128]{1,2,0:T(8,128)}, u32[]{:S(2)}, u32[]{:S(2)}) %all-to-all-start.1) | async-done | bytes 4194336 | tf_op jit(solution)/shard_map/all_to_all | solution.py:36
  170.2 0.0 copy-start.1
  170.2 9.8 %fusion.11 = f32[512,1024]{1,0:T(8,128)S(1)} fusion(f32[512,1024]{1,0:T(8,128)} %all-gather.5.cloned.1.call-done, f32[1024,1024]{0,1:T(8,128)} %bitcast.10), kind=kOutput, calls=%fused_computation.34 | convolution fusion | flops 6442450944 | bytes 8388608 | tf_op jit(solution)/shard_map/dot_general | solution.py:37
  180.0 0.0 copy-done.1
  180.0 9.8 %fusion = f32[512,1024]{1,0:T(8,128)} fusion(f32[1024,1024]{0,1:T(8,128)} %bitcast.10, f32[512,1024]{1,0:T(8,128)S(1)} %copy-done.1, f32[512,1024]{1,0:T(8,128)S(1)} %fusion.11), kind=kOutput, calls=%fused_computation.3 | convolution fusion | flops 6442975232 | bytes 10485760 | tf_op jit(solution)/shard_map/dot_general | solution.py:43
  189.8 0.0 all-reduce.2.cloned.1.call-update
  189.8 0.0 reduce-scatter.2.cloned.1.call-start
  189.9 62.2 %all-reduce.2.cloned.1.call-done = f32[512,1024]{1,0:T(8,128)} async-done(((f32[512,1024]{1,0:T(8,128)}), f32[512,1024]{1,0:T(8,128)}) %all-reduce.2.cloned.1.call-update) | async-done | bytes 2097168 | tf_op jit(solution)/shard_map/psum | solution.py:49
  252.1 1.0 constant_dynamic-slice_fusion
  253.0 0.4 stack.2
  253.4 54.8 %all_to_all.48 = f32[16,512,128]{2,1,0:T(8,128)S(1)} all-to-all(f32[16,512,128]{2,1,0:T(8,128)S(1)} %stack.2), channel_id=1, replica_groups=mesh['row'=16,'col'=8] {'row'}, dimensions={0} | all-to-all | bytes 8388608 | tf_op jit(solution)/shard_map/all_to_all | solution.py:52
  308.2 57.9 %all_to_all.49 = f32[8,1024,128]{2,1,0:T(8,128)} all-to-all(f32[8,1024,128]{2,1,0:T(8,128)S(1)} %bitcast.42), channel_id=1, replica_groups=mesh['row'=16,'col'=8] {'col'}, dimensions={0} | all-to-all | bytes 8388608 | tf_op jit(solution)/shard_map/all_to_all | solution.py:54
  366.1 5.3 %copy.21 = f32[1024,8,128]{0,2,1:T(8,128)} copy(f32[1024,8,128]{2,0,1:T(8,128)} %bitcast.43) | data formatting | bytes 8388608 | tf_op jit(solution)/shard_map/all_to_all | solution.py:54
  371.5 31.0 %negate_bitcast_fusion = f32[2048,1024]{0,1:T(8,128)} fusion(f32[1024,1024]{0,1:T(8,128)} %bitcast.46, f32[2048,1024]{1,0:T(8,128)} %param.7), kind=kOutput, calls=%fused_computation.2 | convolution fusion | flops 25771900928 | bytes 20971520 | tf_op jit(solution)/shard_map/dot_general | solution.py:55
  402.5 0.0 reduce-scatter.2.cloned.1.call-update
  402.5 48.0 %reduce-scatter.2.cloned.1.call-done = f32[2048,128]{0,1:T(8,128)} async-done(((f32[2048,1024]{0,1:T(8,128)}), f32[2048,128]{0,1:T(8,128)}) %reduce-scatter.2.cloned.1.call-update) | async-done | bytes 1048592 | tf_op jit(solution)/shard_map/reduce_scatter | solution.py:58
  450.5 2.5 copy.22
  (9 shorter events, 0.1 us)
Async XLA Ops:
  6.5 21.2 %copy-start = (f32[2048,128]{1,0:T(8,128)S(1)}, f32[2048,128]{1,0:T(8,128)}, u32[]{:S(2)}) copy-start(f32[2048,128]{1,0:T(8,128)} %param.4) | copy-start | bytes 3145732
  31.6 18.0 %all-to-all-start = ((f32[16,64,128]{2,1,0:T(8,128)}), f32[16,64,128]{2,1,0:T(8,128)S(1)}, u32[]{:S(2)}, u32[]{:S(2)}) async-start(f32[16,64,128]{2,1,0:T(8,128)} %broadcast_select_fusion), calls=%async_computation | async-start | bytes 1048576 | tf_op jit(solution)/shard_map/all_to_all | solution.py:29
  39.1 63.2 %all-gather.7.cloned.1.call-start = ((), (), s32[]{:S(2)}) async-start(), calls=%async_computation.8 | async-start | bytes 4456448 | tf_op jit(solution)/shard_map/all_gather | solution.py:35
  51.2 93.3 %all-gather.5.cloned.1.call-start = ((), (), s32[]{:S(2)}) async-start(), calls=%async_computation.7 | async-start | bytes 2359296 | tf_op jit(solution)/shard_map/all_gather | solution.py:34
  107.7 62.5 %all-to-all-start.1 = ((f32[8,1024,128]{1,2,0:T(8,128)}), f32[8,1024,128]{1,2,0:T(8,128)}, u32[]{:S(2)}, u32[]{:S(2)}) async-start(f32[8,1024,128]{1,2,0:T(8,128)} %copy.20), calls=%async_computation.1 | async-start | bytes 8388608 | tf_op jit(solution)/shard_map/all_to_all | solution.py:36
  113.0 139.1 %all-reduce.2.cloned.1.call-start = ((), (), s32[]{:S(2)}) async-start(), calls=%async_computation.5 | async-start | bytes 4194304 | tf_op jit(solution)/shard_map/psum | solution.py:49
  170.2 9.8 %copy-start.1 = (f32[512,1024]{1,0:T(8,128)S(1)}, f32[512,1024]{1,0:T(8,128)}, u32[]{:S(2)}) copy-start(f32[512,1024]{1,0:T(8,128)} %param.6) | copy-start | bytes 6291460
  189.8 260.7 %reduce-scatter.2.cloned.1.call-start = ((), (), s32[]{:S(2)}) async-start(), calls=%async_computation.6 | async-start | bytes 9437184 | tf_op jit(solution)/shard_map/reduce_scatter | solution.py:58
Sparse Core Ops, SparseCore 0:
  51.3 50.9 all-gather.6
  104.0 40.4 all-gather.4
  190.0 62.0 all-reduce.1
  402.6 47.8 reduce-scatter.1
